TPU v7x, 128 devices: a whole 4x4x4 slice. The times are simulated.
128 devices in a mesh: ctx: 32 (over x, z, y_lo), tp: 4 (over y_hi, core).
Axes of the slice: x: 4, y: 4 (y_hi: 2, y_lo: 2; y = y_hi * 2 + y_lo), z: 4, core: 2. Of those that a mesh axis runs over, the one named last changes fastest.
Arguments:
- queries: bfloat16 [1024, 8192], P('ctx', 'tp'), may hold values from -15 to 15
- new_keys: bfloat16 [1024, 1024], P('ctx', 'tp'), may hold values from -6 to 6
- new_values: bfloat16 [1024, 1024], P('ctx', 'tp'), may hold values from -6 to 6
- cache_keys: bfloat16 [131072, 1024], P('ctx', 'tp'), may hold values from -6 to 6
- cache_values: bfloat16 [131072, 1024], P('ctx', 'tp'), may hold values from -6 to 6
- keep_tiles: int32 [32, 8, 24], P('ctx', 'tp'), may hold values from 0 to 31, as said below
- tile_count: int32 [32, 8], P('ctx', 'tp'), may hold values from 1 to 24
- owner_slot: int32 [32], replicated, may hold values from 0 to 31, each once
- out_weight: bfloat16 [8192, 8192], P('tp', 'ctx'), may hold values from -0.0625 to 0.0625
Outputs:
- projected_out: float32 [1024, 8192], P('tp', 'ctx')
Inputs may be any that keep to these rules, and one draw needn't show every extreme that they name: `keep_tiles`: the 24 entries of each keep list are distinct tile numbers; entries at or past tile_count are ignored.
All inputs are finite; a program needn't handle non-finite values.
Results may differ from a plain program's by a relative error of at most 0.0055.
Values may be sent and summed in bfloat16 or wider, within the bound.
A program may use at most 128 MiB of HBM per device.

v0:
```python
import jax
import jax.numpy as jnp
from jax import lax
from jax.sharding import PartitionSpec as P

DH = 128
TILE = 128
TB = 4
NEG_INF = -jnp.inf


def fold_scores(state_now, scores, value_rows):
    run_max, run_total, run_sum = state_now
    new_max = jnp.maximum(run_max, jnp.max(scores, axis=-1))
    shrink = jnp.exp(run_max - new_max)
    weights = jnp.exp(scores - new_max[..., None])
    run_total = run_total * shrink + jnp.sum(weights, axis=-1)
    mixture = jnp.einsum(
        "rhk,kd->rhd", weights.astype(jnp.bfloat16), value_rows, preferred_element_type=jnp.float32
    )
    run_sum = run_sum * shrink[..., None] + mixture
    return (new_max, run_total, run_sum)


def body(
    queries,
    new_keys,
    new_values,
    cache_keys,
    cache_values,
    keep_tiles,
    tile_count,
    owner_slot,
    out_weight,
):
    q_dev = queries.shape[0]
    kv_local = new_keys.shape[1] // DH
    q_local = queries.shape[1] // DH
    group_size = q_local // kv_local
    ctx_count = lax.axis_size("ctx")
    total_rows = q_dev * ctx_count
    my_index = lax.axis_index("ctx")
    score_scale = DH ** (-0.5)
    slot_count = keep_tiles.shape[2]
    key_place = owner_slot[my_index] * q_dev + jnp.arange(q_dev, dtype=jnp.int32)
    tiled_keys = cache_keys.reshape(-1, TILE, kv_local, DH)
    tiled_values = cache_values.reshape(-1, TILE, kv_local, DH)
    kept_keys = [
        jnp.take(tiled_keys[:, :, kv_head, :], keep_tiles[0, kv_head], axis=0)
        for kv_head in range(kv_local)
    ]
    kept_values = [
        jnp.take(tiled_values[:, :, kv_head, :], keep_tiles[0, kv_head], axis=0)
        for kv_head in range(kv_local)
    ]
    query_rows = lax.all_gather(queries, "ctx", axis=0, tiled=True)
    row_count = query_rows.shape[0]
    row_ids = jnp.arange(row_count, dtype=jnp.int32)
    query_place = owner_slot[row_ids // q_dev] * q_dev + row_ids % q_dev
    causal = query_place[:, None] >= key_place[None, :]
    pieces_max = []
    pieces_total = []
    pieces_sum = []
    for kv_head in range(kv_local):
        query_head = query_rows[
            :, kv_head * group_size * DH : (kv_head + 1) * group_size * DH
        ].reshape(row_count, group_size, DH)
        start_state = (
            jnp.full((row_count, group_size), NEG_INF, jnp.float32),
            jnp.zeros((row_count, group_size), jnp.float32),
            jnp.zeros((row_count, group_size, DH), jnp.float32),
        )
        live_count = tile_count[0, kv_head]

        def tile_block(
            block_id, state_inner, kv_head=kv_head, query_head=query_head, live_count=live_count
        ):
            key_block = lax.dynamic_slice_in_dim(kept_keys[kv_head], block_id * TB, TB, 0).reshape(
                TB * TILE, DH
            )
            value_block = lax.dynamic_slice_in_dim(
                kept_values[kv_head], block_id * TB, TB, 0
            ).reshape(TB * TILE, DH)
            tile_ids = block_id * TB + jnp.arange(TB, dtype=jnp.int32)
            live_keys = jnp.repeat(tile_ids < live_count, TILE)
            scores = (
                jnp.einsum("rhd,kd->rhk", query_head, key_block, preferred_element_type=jnp.float32)
                * score_scale
            )
            scores = jnp.where(live_keys[None, None, :], scores, NEG_INF)
            return fold_scores(state_inner, scores, value_block)

        block_limit = slot_count // TB
        state_head = lax.fori_loop(0, block_limit, tile_block, start_state)
        fresh_keys = new_keys[:, kv_head * DH : (kv_head + 1) * DH]
        fresh_values = new_values[:, kv_head * DH : (kv_head + 1) * DH]
        scores = (
            jnp.einsum("rhd,kd->rhk", query_head, fresh_keys, preferred_element_type=jnp.float32)
            * score_scale
        )
        scores = jnp.where(causal[:, None, :], scores, NEG_INF)
        head_max, head_total, head_sum = fold_scores(state_head, scores, fresh_values)
        pieces_max.append(head_max)
        pieces_total.append(head_total)
        pieces_sum.append(head_sum.reshape(row_count, group_size * DH))
    maxima_all = jnp.concatenate(pieces_max, axis=1)
    totals_all = jnp.concatenate(pieces_total, axis=1)
    sums_all = jnp.concatenate(pieces_sum, axis=1)
    top_max = lax.pmax(maxima_all, "ctx")
    factor = jnp.exp(maxima_all - top_max)
    scaled = (sums_all.reshape(total_rows, q_local, DH) * factor[..., None]).reshape(
        total_rows, q_local * DH
    )
    numerator, denominator = (
        lax.psum_scatter(scaled, "ctx", scatter_dimension=0, tiled=True),
        lax.psum_scatter(totals_all * factor, "ctx", scatter_dimension=0, tiled=True),
    )
    attn_rows = (
        (numerator.reshape(q_dev, q_local, DH) / denominator[..., None])
        .reshape(q_dev, q_local * DH)
        .astype(jnp.bfloat16)
    )
    projected = jnp.dot(
        lax.all_gather(attn_rows, "ctx", axis=0, tiled=True),
        out_weight,
        preferred_element_type=jnp.float32,
    )
    return lax.psum_scatter(projected, "tp", scatter_dimension=0, tiled=True)


def solution(mesh):
    return jax.shard_map(
        body,
        mesh=mesh,
        in_specs=(
            P("ctx", "tp"),
            P("ctx", "tp"),
            P("ctx", "tp"),
            P("ctx", "tp"),
            P("ctx", "tp"),
            P("ctx", "tp", None),
            P("ctx", "tp"),
            P(),
            P("tp", "ctx"),
        ),
        out_specs=P("tp", "ctx"),
        check_vma=False,
    )
```

profile of v0, /device:TPU:1, one launch (start us, length us, event | category | flops | bytes accessed | tf_op | source)
XLA Modules:
  0.0 1224.2 jit_solution(18363022142407999071)
XLA Ops:
  14.0 6.1 fusion.48
  43.7 15.2 %fusion.43 = s32[1024]{0:T(1024)S(1)} fusion(pred[1024]{0:T(1024)(128)(4,1)S(1)} %compare_reduce_fusion, pred[1024]{0:T(1024)(128)(4,1)S(1)} %compare_reduce_fusion.1, pred[1024]{0:T(1024)(128)(4,1)S(1)} %compare_reduce_fusion.2, pred[1024]{0:T(1024)(128)(4,1)S(1)} %compare_reduce_fusion.3, pred[1024]{0:T(1024)(128)(4,1)S(1)} %compare_reduce_fusion.4, ...), kind=kLoop, calls=%fused_computation.122 | loop fusion | flops 33792 | bytes 33892 | tf_op jit(solution)/shard_map/add | solution.py:59
  64.2 85.2 %all-gather.3.cloned.1.call-done = bf16[1024,2048]{1,0:T(8,128)(2,1)} async-done(((bf16[32,2048]{1,0:T(8,128)(2,1)}), bf16[1024,2048]{1,0:T(8,128)(2,1)}) %all-gather.3.cloned.1.call-update) | async-done | bytes 4194320 | tf_op jit(solution)/shard_map/all_gather | solution.py:56
  172.9 103.2 %while.37 = (s32[]{:T(128)}, f32[1024,8]{0,1:T(8,128)S(1)}, f32[1024,8]{0,1:T(8,128)S(1)}, f32[1024,8,128]{2,0,1:T(8,128)}, s32[]{:T(128)}, /*index=5*/bf16[24,1...) while((s32[]{:T(128)}, f32[1024,8]{0,1:T(8,128)S(1)}, ...), condition=%wide.region_8.10_spmd.clone, body=%wide.region_5.9_spmd.clone.sunk | while | flops 2196807680 | bytes 62130376 | solution.py:94
  182.4 6.3 fusion.93
  198.3 7.9 fusion.93
  215.8 7.9 fusion.93
  233.3 7.9 fusion.93
  250.7 7.9 fusion.93
  268.2 7.9 fusion.93
  281.4 93.2 %while.36 = (s32[]{:T(128)}, f32[1024,8]{0,1:T(8,128)S(1)}, f32[1024,8]{0,1:T(8,128)S(1)}, f32[1024,8,128]{2,0,1:T(8,128)}, s32[]{:T(128)}, /*index=5*/bf16[24,1...) while((s32[]{:T(128)}, f32[1024,8]{0,1:T(8,128)S(1)}, ...), condition=%wide.region_3.5_spmd.clone, body=%wide.region_0.4_spmd.clone.sunk | while | flops 2196807680 | bytes 62130376 | solution.py:94
  289.3 6.3 fusion.86
  303.6 7.9 fusion.86
  319.4 7.9 fusion.86
  335.2 7.9 fusion.86
  350.9 7.9 fusion.86
  366.7 7.9 fusion.86
  389.6 269.2 %all-reduce.2.cloned.1.call-done = f32[1024,16]{0,1:T(8,128)} async-done(((f32[1024,16]{0,1:T(8,128)}), f32[1024,16]{0,1:T(8,128)}) %all-reduce.2.cloned.1.call-update) | async-done | bytes 65552 | tf_op jit(solution)/shard_map/pmax | solution.py:109
  660.8 8.7 maximum_multiply_fusion
  669.4 9.1 copy.61
  678.7 130.2 %reduce-scatter.12.cloned.1.call-done = f32[32,16]{1,0:T(8,128)} async-done(((f32[1024,16]{1,0:T(8,128)}), f32[32,16]{1,0:T(8,128)}) %reduce-scatter.12.cloned.1.call-update) | async-done | bytes 2064
  809.7 209.7 %reduce-scatter.10.cloned.1.call-done = f32[32,2048]{1,0:T(8,128)} async-done(((f32[1024,2048]{1,0:T(8,128)}), f32[32,2048]{1,0:T(8,128)}) %reduce-scatter.10.cloned.1.call-update) | async-done | bytes 262160
  1021.7 138.5 %all-gather.5.cloned.1.call-done = bf16[1024,2048]{1,0:T(8,128)(2,1)} async-done(((bf16[32,2048]{1,0:T(8,128)(2,1)}), bf16[1024,2048]{1,0:T(8,128)(2,1)}) %all-gather.5.cloned.1.call-update) | async-done | bytes 4194320 | tf_op jit(solution)/shard_map/all_gather | solution.py:124
  1164.6 52.8 %reduce-scatter.8.cloned.1.call-done = f32[256,256]{1,0:T(8,128)} async-done(((f32[1024,256]{1,0:T(8,128)}), f32[256,256]{1,0:T(8,128)}) %reduce-scatter.8.cloned.1.call-update) | async-done | bytes 262160 | tf_op jit(solution)/shard_map/reduce_scatter | solution.py:128
  (211 shorter events, 193.3 us)
Async XLA Ops:
  6.5 1153.6 %copy-start = (bf16[2048,256]{1,0:T(8,128)(2,1)S(1)}, bf16[2048,256]{1,0:T(8,128)(2,1)}, u32[]{:S(2)}) copy-start(bf16[2048,256]{1,0:T(8,128)(2,1)} %param.23) | copy-start | bytes 3145732
  6.5 142.9 %all-gather.3.cloned.1.call-start = ((), (), s32[]{:S(2)}) async-start(), calls=%async_computation.3 | async-start | bytes 4325376 | tf_op jit(solution)/shard_map/all_gather | solution.py:56
  7.3 651.6 %all-reduce.2.cloned.1.call-start = ((), (), s32[]{:S(2)}) async-start(), calls=%async_computation.4 | async-start | bytes 131072 | tf_op jit(solution)/shard_map/pmax | solution.py:109
  7.4 6.6 copy-start.13
  28.5 4.2 copy-start.5
  28.5 7.3 copy-start.7
  28.5 14.5 %copy-start.12 = (s32[1,2]{1,0:T(1,128)S(1)}, s32[1,2]{1,0:T(1,128)}, u32[]{:S(2)}) copy-start(s32[1,2]{1,0:T(1,128)} %param.21) | copy-start | bytes 28
  34.3 27.5 %copy-start.6 = (bf16[24,128,128]{2,1,0:T(8,128)(2,1)S(1)}, bf16[24,128,128]{2,1,0:T(8,128)(2,1)}, u32[]{:S(2)}) copy-start(bf16[24,128,128]{2,1,0:T(8,128)(2,1)} %gather_fusion.1) | copy-start | bytes 2359300
  156.1 7.0 copy-start.10
  163.1 3.9 copy-start.1
  374.6 5.5 copy-start.9
  374.6 5.5 copy-start.4
  374.6 5.8 copy-start.8
  374.6 6.4 copy-start.3
  374.6 6.7 copy-start.11
  381.3 427.6 %reduce-scatter.12.cloned.1.call-start = ((), (), s32[]{:S(2)}) async-start(), calls=%async_computation.8 | async-start | bytes 540672
  381.4 5.5 copy-start.2
  660.7 358.6 %reduce-scatter.10.cloned.1.call-start = ((), (), s32[]{:S(2)}) async-start(), calls=%async_computation.7 | async-start | bytes 8650752
  678.6 481.6 %all-gather.5.cloned.1.call-start = ((), (), s32[]{:S(2)}) async-start(), calls=%async_computation.5 | async-start | bytes 4325376 | tf_op jit(solution)/shard_map/all_gather | solution.py:124
  1021.6 195.8 %reduce-scatter.8.cloned.1.call-start = ((), (), s32[]{:S(2)}) async-start(), calls=%async_computation.6 | async-start | bytes 1310720 | tf_op jit(solution)/shard_map/reduce_scatter | solution.py:128
Sparse Core Ops, SparseCore 0:
  9.0 140.3 all-gather.2
  381.4 277.4 all-reduce.1
  661.3 147.4 reduce-scatter.11
  811.1 208.1 reduce-scatter.9
  1021.7 138.3 all-gather.4
  1164.7 52.6 reduce-scatter.7
where the time goes:
time: 1230 us; the launch traced here: 1220 us
  waiting for transfers between devices  886 us (72%)
  matrix products  148 us (12%)
  other arithmetic  90.1 us (7%)
  local copies, waits for them, and re-layouts  84.6 us (7%)
  between operations  14.4 us (1%)
    unnamed x8, waiting for transfers between devices  341 us
    pmax x1, waiting for transfers between devices, body(): top_max = lax.pmax(maxima_all, 'ctx')  269 us
    all_gather x1, waiting for transfers between devices, body(): lax.all_gather(attn_rows, 'ctx', axis=0, tiled=True)  139 us
    dot_general x14, matrix products, fold_scores(): jnp.einsum('rhk,kd->rhd', weights.astype(jnp.bfloat16), value_rows, prefe...  99.5 us
    all_gather x1, waiting for transfers between devices, body(): query_rows = lax.all_gather(queries, 'ctx', axis=0, tiled=True)  85.2 us
    reduce_scatter x1, waiting for transfers between devices, body(): return lax.psum_scatter(projected, 'tp', scatter_dimension=0, tiled=True)  52.8 us
    reduce_sum x14, other arithmetic, fold_scores(): run_total = run_total * shrink + jnp.sum(weights, axis=-1)  45.9 us
    dot_general x12, matrix products, tile_block(): jnp.einsum('rhd,kd->rhk', query_head, key_block, preferred_element_type=j...  38.1 us
  transfers between devices with their start and end apart: 6, of which 6 were waited for; matrix products, arithmetic and copies ran while one was open for 7% of the time, Pallas kernels for 0%

commit v1 on v0

--- a/solution.py
+++ b/solution.py
@@ -2,11 +2,25 @@
 import jax.numpy as jnp
 from jax import lax
 from jax.sharding import PartitionSpec as P
+from jax.lax import all_to_all, axis_size
 
 DH = 128
 TILE = 128
 TB = 4
 NEG_INF = -jnp.inf
+
+
+def _replace_desk(sheet):
+    front = jnp.concatenate(
+        all_to_all(
+            jnp.stack([sheet] * axis_size("ctx"), axis=0),
+            axis_name="ctx",
+            split_axis=0,
+            concat_axis=0,
+        ),
+        0,
+    )
+    return front
 
 
 def fold_scores(state_now, scores, value_rows):
@@ -120,11 +134,7 @@
         .reshape(q_dev, q_local * DH)
         .astype(jnp.bfloat16)
     )
-    projected = jnp.dot(
-        lax.all_gather(attn_rows, "ctx", axis=0, tiled=True),
-        out_weight,
-        preferred_element_type=jnp.float32,
-    )
+    projected = jnp.dot(_replace_desk(attn_rows), out_weight, preferred_element_type=jnp.float32)
     return lax.psum_scatter(projected, "tp", scatter_dimension=0, tiled=True)
 
 

time: 1230 us -> 1120 us (0.911)
  waiting for transfers between devices: 886 us -> 727 us
  blocking collectives: 0 us -> 56.6 us
    all_gather x1 -> x0, waiting for transfers between devices: 139 us -> none  [body(): lax.all_gather(attn_rows, 'ctx', axis=0, tiled=True)]
    all_to_all x0 -> x1, blocking collectives: none -> 56.6 us  [_replace_desk(): all_to_all(jnp.stack([sheet] * axis_size('ctx'), axis=0), axis_name='ctx'...]
    reduce_scatter x1, waiting for transfers between devices: 52.8 us -> 31.7 us  [body(): return lax.psum_scatter(projected, 'tp', scatter_dimension=0, tiled=True)]
    unnamed x8 -> x7, waiting for transfers between devices: 341 us -> 341 us
  transfers between devices with their start and end apart: 6 -> 5, of which waited for: 6 -> 5; matrix products, arithmetic and copies ran while one was open for 7% -> 7% of each run, Pallas kernels for 0% -> 0%
where the time goes in v1:
time: 1120 us
  waiting for transfers between devices  727 us (65%)
  matrix products  146 us (13%)
  other arithmetic  90.1 us (8%)
  local copies, waits for them, and re-layouts  84.5 us (8%)
  blocking collectives  56.6 us (5%)
  between operations  14.1 us (1%)
    unnamed x7, waiting for transfers between devices  341 us
    pmax x1, waiting for transfers between devices, body(): top_max = lax.pmax(maxima_all, 'ctx')  269 us
    dot_general x14, matrix products, fold_scores(): jnp.einsum('rhk,kd->rhd', weights.astype(jnp.bfloat16), value_rows, prefe...  99.5 us
    all_gather x1, waiting for transfers between devices, body(): query_rows = lax.all_gather(queries, 'ctx', axis=0, tiled=True)  85.2 us
    all_to_all x1, blocking collectives, _replace_desk(): all_to_all(jnp.stack([sheet] * axis_size('ctx'), axis=0), axis_name='ctx'...  56.6 us
    reduce_sum x14, other arithmetic, fold_scores(): run_total = run_total * shrink + jnp.sum(weights, axis=-1)  45.9 us
    dot_general x12, matrix products, tile_block(): jnp.einsum('rhd,kd->rhk', query_head, key_block, preferred_element_type=j...  38.1 us
    reduce_scatter x1, waiting for transfers between devices, body(): return lax.psum_scatter(projected, 'tp', scatter_dimension=0, tiled=True)  31.7 us
  transfers between devices with their start and end apart: 5, of which 5 were waited for; matrix products, arithmetic and copies ran while one was open for 7% of the time, Pallas kernels for 0%

profile of v1, /device:TPU:1, one launch (start us, length us, event | category | flops | bytes accessed | tf_op | source)
XLA Modules:
  0.0 1118.6 jit_solution(8841613759781395432)
XLA Ops:
  14.0 6.1 fusion.48
  43.7 15.2 %fusion.43 = s32[1024]{0:T(1024)S(1)} fusion(pred[1024]{0:T(1024)(128)(4,1)S(1)} %compare_reduce_fusion, pred[1024]{0:T(1024)(128)(4,1)S(1)} %compare_reduce_fusion.1, pred[1024]{0:T(1024)(128)(4,1)S(1)} %compare_reduce_fusion.2, pred[1024]{0:T(1024)(128)(4,1)S(1)} %compare_reduce_fusion.3, pred[1024]{0:T(1024)(128)(4,1)S(1)} %compare_reduce_fusion.4, ...), kind=kLoop, calls=%fused_computation.122 | loop fusion | flops 33792 | bytes 33892 | tf_op jit(solution)/shard_map/add | solution.py:73
  64.2 85.2 %all-gather.2.cloned.1.call-done = bf16[1024,2048]{1,0:T(8,128)(2,1)} async-done(((bf16[32,2048]{1,0:T(8,128)(2,1)}), bf16[1024,2048]{1,0:T(8,128)(2,1)}) %all-gather.2.cloned.1.call-update) | async-done | bytes 4194320 | tf_op jit(solution)/shard_map/all_gather | solution.py:70
  172.9 103.2 %while.37 = (s32[]{:T(128)}, f32[1024,8]{0,1:T(8,128)S(1)}, f32[1024,8]{0,1:T(8,128)S(1)}, f32[1024,8,128]{2,0,1:T(8,128)}, s32[]{:T(128)}, /*index=5*/bf16[24,1...) while((s32[]{:T(128)}, f32[1024,8]{0,1:T(8,128)S(1)}, ...), condition=%wide.region_8.10_spmd.clone, body=%wide.region_5.9_spmd.clone.sunk | while | flops 2196807680 | bytes 62130376 | solution.py:108
  182.4 6.3 fusion.93
  198.3 7.9 fusion.93
  215.8 7.9 fusion.93
  233.3 7.9 fusion.93
  250.7 7.9 fusion.93
  268.2 7.9 fusion.93
  281.4 93.2 %while.36 = (s32[]{:T(128)}, f32[1024,8]{0,1:T(8,128)S(1)}, f32[1024,8]{0,1:T(8,128)S(1)}, f32[1024,8,128]{2,0,1:T(8,128)}, s32[]{:T(128)}, /*index=5*/bf16[24,1...) while((s32[]{:T(128)}, f32[1024,8]{0,1:T(8,128)S(1)}, ...), condition=%wide.region_3.5_spmd.clone, body=%wide.region_0.4_spmd.clone.sunk | while | flops 2196807680 | bytes 62130376 | solution.py:108
  289.3 6.3 fusion.86
  303.6 7.9 fusion.86
  319.4 7.9 fusion.86
  335.2 7.9 fusion.86
  350.9 7.9 fusion.86
  366.7 7.9 fusion.86
  389.6 269.2 %all-reduce.2.cloned.1.call-done = f32[1024,16]{0,1:T(8,128)} async-done(((f32[1024,16]{0,1:T(8,128)}), f32[1024,16]{0,1:T(8,128)}) %all-reduce.2.cloned.1.call-update) | async-done | bytes 65552 | tf_op jit(solution)/shard_map/pmax | solution.py:123
  660.8 8.7 maximum_multiply_fusion
  669.4 9.1 copy.64
  678.7 130.2 %reduce-scatter.12.cloned.1.call-done = f32[32,16]{1,0:T(8,128)} async-done(((f32[1024,16]{1,0:T(8,128)}), f32[32,16]{1,0:T(8,128)}) %reduce-scatter.12.cloned.1.call-update) | async-done | bytes 2064
  809.7 209.7 %reduce-scatter.10.cloned.1.call-done = f32[32,2048]{1,0:T(8,128)} async-done(((f32[1024,2048]{1,0:T(8,128)}), f32[32,2048]{1,0:T(8,128)}) %reduce-scatter.10.cloned.1.call-update) | async-done | bytes 262160
  1021.5 56.6 %all_to_all.5 = bf16[32,32,2048]{2,1,0:T(8,128)(2,1)S(1)} all-to-all(bf16[32,32,2048]{2,1,0:T(8,128)(2,1)S(1)} %stack.2), channel_id=1, replica_groups=mesh['ctx'=32,'tp'=4] {'ctx'}, dimensions={0} | all-to-all | bytes 8388608 | tf_op jit(solution)/shard_map/all_to_all | solution.py:15
  1080.3 31.7 %reduce-scatter.8.cloned.1.call-done = f32[256,256]{1,0:T(8,128)} async-done(((f32[1024,256]{1,0:T(8,128)}), f32[256,256]{1,0:T(8,128)}) %reduce-scatter.8.cloned.1.call-update) | async-done | bytes 262160 | tf_op jit(solution)/shard_map/reduce_scatter | solution.py:138
  (210 shorter events, 191.0 us)
Async XLA Ops:
  6.5 1071.5 %copy-start = (bf16[2048,256]{1,0:T(8,128)(2,1)S(1)}, bf16[2048,256]{1,0:T(8,128)(2,1)}, u32[]{:S(2)}) copy-start(bf16[2048,256]{1,0:T(8,128)(2,1)} %param.23) | copy-start | bytes 3145732
  6.5 142.9 %all-gather.2.cloned.1.call-start = ((), (), s32[]{:S(2)}) async-start(), calls=%async_computation.4 | async-start | bytes 4325376 | tf_op jit(solution)/shard_map/all_gather | solution.py:70
  7.3 651.6 %all-reduce.2.cloned.1.call-start = ((), (), s32[]{:S(2)}) async-start(), calls=%async_computation.5 | async-start | bytes 131072 | tf_op jit(solution)/shard_map/pmax | solution.py:123
  7.4 6.6 copy-start.13
  28.5 4.2 copy-start.5
  28.5 7.3 copy-start.7
  28.5 14.5 %copy-start.12 = (s32[1,2]{1,0:T(1,128)S(1)}, s32[1,2]{1,0:T(1,128)}, u32[]{:S(2)}) copy-start(s32[1,2]{1,0:T(1,128)} %param.21) | copy-start | bytes 28
  34.3 27.5 %copy-start.6 = (bf16[24,128,128]{2,1,0:T(8,128)(2,1)S(1)}, bf16[24,128,128]{2,1,0:T(8,128)(2,1)}, u32[]{:S(2)}) copy-start(bf16[24,128,128]{2,1,0:T(8,128)(2,1)} %gather_fusion.1) | copy-start | bytes 2359300
  156.1 7.0 copy-start.10
  163.1 3.9 copy-start.1
  374.6 5.5 copy-start.9
  374.6 5.5 copy-start.4
  374.6 5.8 copy-start.8
  374.6 6.4 copy-start.3
  374.6 6.7 copy-start.11
  381.3 427.6 %reduce-scatter.12.cloned.1.call-start = ((), (), s32[]{:S(2)}) async-start(), calls=%async_computation.8 | async-start | bytes 540672
  381.4 5.5 copy-start.2
  660.7 358.6 %reduce-scatter.10.cloned.1.call-start = ((), (), s32[]{:S(2)}) async-start(), calls=%async_computation.7 | async-start | bytes 8650752
  678.6 433.4 %reduce-scatter.8.cloned.1.call-start = ((), (), s32[]{:S(2)}) async-start(), calls=%async_computation.6 | async-start | bytes 1310720 | tf_op jit(solution)/shard_map/reduce_scatter | solution.py:138
Sparse Core Ops, SparseCore 0:
  9.0 140.3 all-gather.1
  381.4 277.4 all-reduce.1
  661.3 147.4 reduce-scatter.11
  811.1 208.1 reduce-scatter.9
  1080.5 31.5 reduce-scatter.7
